TPU v7x, 256 devices: a whole 4x4x8 slice. The times are simulated.
256 devices in a mesh: gx: 4 (over y), gy: 4 (over z_hi, core), gz: 16 (over z_lo, x).
Axes of the slice: x: 4, y: 4, z: 8 (z_hi: 2, z_lo: 4; z = z_hi * 4 + z_lo), core: 2. Of those that a mesh axis runs over, the one named last changes fastest.
Arguments:
- currents: float32 [131072, 512], P(('gx', 'gy', 'gz')), may hold values from -6 to 6
Outputs:
- power_spectra: float32 [256, 512, 512], P(('gx', 'gy', 'gz'))
- cross_spectra: float32 [256, 512, 512], P(('gx', 'gy', 'gz'))
All inputs are finite; a program needn't handle non-finite values.
Results may differ from a plain program's by a relative error of at most 0.00014.
Values sent between devices are 32-bit elements; how exact they have to be, the bound alone decides.
A program may use at most 64 MiB of HBM per device.

v0:
```python
import math

import jax
import jax.numpy as jnp
import numpy as np
from jax import lax
from jax.sharding import PartitionSpec as P

BIN_WIDTH = 256


PRECISE = lax.Precision.HIGHEST


def swapped(block, axis, distance):
    count = lax.axis_size(axis)
    route = []
    for low in range(count):
        high = low | 1 << distance
        if high != low and high < count:
            route += [(low, high), (high, low)]
    return lax.ppermute(block, axis, route)


def cos_sin(numerator, period):
    phase_angle = 2.0 * math.pi / period * numerator.astype(jnp.float32)
    return (jnp.cos(phase_angle), jnp.sin(phase_angle))


def dft_tables(length):
    row_index = lax.broadcasted_iota(jnp.int32, (length, length), 0)
    col_index = lax.broadcasted_iota(jnp.int32, (length, length), 1)
    return cos_sin(row_index * col_index % length, length)


def reverse_bits(number_in, bit_count):
    result = number_in * 0
    for bit_index in range(bit_count):
        result = result + ((number_in >> bit_index & 1) << bit_count - 1 - bit_index)
    return result


def rotate(real_part, imag_part, cosine, sine_part):
    return (real_part * cosine + imag_part * sine_part, imag_part * cosine - real_part * sine_part)


def recover(z_real, z_imag, m_real, m_imag, frequency, steps_total):
    even_real = 0.5 * (z_real + m_real)
    even_imag = 0.5 * (z_imag - m_imag)
    odd_real = 0.5 * (z_imag + m_imag)
    odd_imag = -0.5 * (z_real - m_real)
    cosine, sine_part = cos_sin(frequency, steps_total)
    return (
        even_real + cosine * odd_real + sine_part * odd_imag,
        even_imag + cosine * odd_imag - sine_part * odd_real,
    )


def spectra(real_part, imag_part, einsum_form, steps_total):
    scaling = 1.0 / (float(steps_total) * float(BIN_WIDTH))
    power_sum = jnp.einsum(einsum_form, real_part, real_part, precision=PRECISE)
    power_sum = power_sum + jnp.einsum(einsum_form, imag_part, imag_part, precision=PRECISE)
    cross_sum = jnp.einsum(einsum_form, imag_part, real_part, precision=PRECISE)
    return (power_sum * scaling, (cross_sum - jnp.swapaxes(cross_sum, 1, 2)) * scaling)


def combine_pair(series, partner, device_index, global_bit):
    half_span = 1 << global_bit
    upper_half = device_index >> global_bit & 1
    offset_in = device_index & half_span - 1
    phase_angle = math.pi / half_span * offset_in.astype(jnp.float32)
    cosine = jnp.cos(phase_angle)
    sine_part = jnp.sin(phase_angle)
    difference = partner - series
    turned = jnp.stack(
        [
            difference[:, 0] * cosine + difference[:, 1] * sine_part,
            difference[:, 1] * cosine - difference[:, 0] * sine_part,
        ],
        axis=1,
    )
    return jnp.where(upper_half == 1, turned, series + partner)


def by_sections(currents, device_index):
    steps_local, width = currents.shape
    half = steps_local // 2
    devices = lax.axis_size(("gx", "gy", "gz"))
    bits_high = lax.axis_size("gx").bit_length() - 1
    bits_mid = lax.axis_size("gy").bit_length() - 1
    bits_low = lax.axis_size("gz").bit_length() - 1
    total_bits = bits_high + bits_mid + bits_low
    series = currents.reshape(half, 2, width)
    for bit_index in reversed(range(bits_high)):
        partner = swapped(series, "gx", bit_index)
        series = combine_pair(series, partner, device_index, bit_index + bits_mid + bits_low)
    for bit_index in reversed(range(bits_mid)):
        partner = swapped(series, "gy", bit_index)
        series = combine_pair(series, partner, device_index, bit_index + bits_low)
    for bit_index in reversed(range(bits_low)):
        partner = swapped(series, "gz", bit_index)
        series = combine_pair(series, partner, device_index, bit_index)
    q_class = reverse_bits(device_index, total_bits)
    blocks = half * devices
    steps_total = 2 * blocks
    step_index = lax.broadcasted_iota(jnp.int32, (half, 1), 0)
    cosine, sine_part = cos_sin(step_index * q_class, blocks)
    twisted_real, twisted_imag = rotate(series[:, 0], series[:, 1], cosine, sine_part)
    cos_table, sin_table = dft_tables(half)
    stacked = jnp.stack([twisted_real, twisted_imag], axis=1)
    with_cos = jnp.einsum("jm,mkn->jkn", cos_table, stacked, precision=PRECISE)
    with_sin = jnp.einsum("jm,mkn->jkn", sin_table, stacked, precision=PRECISE)
    spectrum = jnp.stack([with_cos[:, 0] + with_sin[:, 1], with_cos[:, 1] - with_sin[:, 0]], axis=1)
    reversed_rows = spectrum[::-1]
    mirrored = jnp.where(q_class == 0, jnp.roll(reversed_rows, 1, axis=0), reversed_rows)
    wide_count = lax.axis_size("gx") * lax.axis_size("gy")
    narrow_count = lax.axis_size("gz")
    per_block = half // devices
    shape_out = (wide_count, narrow_count, per_block, 2, width)
    got_spec, got_mirror = (
        lax.all_to_all(
            lax.all_to_all(
                spectrum.reshape(shape_out), ("gx", "gy"), split_axis=0, concat_axis=0, tiled=True
            ),
            "gz",
            split_axis=1,
            concat_axis=1,
            tiled=True,
        ),
        lax.all_to_all(
            lax.all_to_all(
                mirrored.reshape(shape_out), ("gx", "gy"), split_axis=0, concat_axis=0, tiled=True
            ),
            "gz",
            split_axis=1,
            concat_axis=1,
            tiled=True,
        ),
    )
    got_spec = got_spec.reshape(devices, per_block, 2, width)
    got_mirror = got_mirror.reshape(devices, per_block, 2, width)
    source_class = reverse_bits(np.arange(devices), total_bits)
    partner_source = reverse_bits((devices - source_class) % devices, total_bits)
    got_mirror = jnp.take(got_mirror, jnp.asarray(partner_source.astype(np.int32)), axis=0)
    row_offset = lax.broadcasted_iota(jnp.int32, (devices, per_block, 1), 1)
    class_column = jnp.asarray(source_class.astype(np.int32)).reshape(devices, 1, 1)
    frequency = devices * (device_index * per_block + row_offset) + class_column
    x_real, x_imag = recover(
        got_spec[:, :, 0],
        got_spec[:, :, 1],
        got_mirror[:, :, 0],
        got_mirror[:, :, 1],
        frequency,
        steps_total,
    )
    per_bin = BIN_WIDTH // devices
    bins_here = per_block // per_bin
    return spectra(
        x_real.reshape(devices, bins_here, per_bin, width),
        x_imag.reshape(devices, bins_here, per_bin, width),
        "pbrm,pbrn->bmn",
        steps_total,
    )


def on_device(currents):
    return by_sections(currents, lax.axis_index(("gx", "gy", "gz")))


def solution(mesh):
    return jax.shard_map(
        on_device,
        mesh=mesh,
        in_specs=(P(("gx", "gy", "gz"), None),),
        out_specs=(P(("gx", "gy", "gz"), None, None), P(("gx", "gy", "gz"), None, None)),
        check_vma=False,
    )
```

profile of v0, /device:TPU:64, one launch (start us, length us, event | category | flops | bytes accessed | tf_op | source)
XLA Modules:
  0.0 394.7 jit_solution(15324333766194468331)
XLA Ops:
  0.6 1.8 reshape.165
  2.7 3.3 collective-permute-start
  6.1 23.0 %collective-permute-done = f32[256,2,512]{2,0,1:T(8,128)S(1)} collective-permute-done((f32[256,2,512]{2,0,1:T(8,128)S(1)}, f32[256,2,512]{2,0,1:T(8,128)S(1)}, u32[]{:S(2)}, u32[]{:S(2)}) %collective-permute-start) | collective-permute-done | bytes 1048608 | tf_op jit(solution)/shard_map/ppermute | solution.py:22
  30.0 1.7 collective-permute-start.1
  31.8 22.3 %collective-permute-done.1 = f32[256,2,512]{2,0,1:T(8,128)S(1)} collective-permute-done((f32[256,2,512]{2,0,1:T(8,128)S(1)}, f32[256,2,512]{2,0,1:T(8,128)S(1)}, u32[]{:S(2)}, u32[]{:S(2)}) %collective-permute-start.1) | collective-permute-done | bytes 1048608 | tf_op jit(solution)/shard_map/ppermute | solution.py:22
  54.9 5.5 %collective-permute-start.2 = (f32[256,2,512]{2,0,1:T(8,128)S(1)}, f32[256,2,512]{2,0,1:T(8,128)S(1)}, u32[]{:S(2)}, u32[]{:S(2)}) collective-permute-start(f32[256,2,512]{2,0,1:T(8,128)S(1)} %maximum_select_fusion.1), channel_id=1, source_target_pairs={{0,32},{32,0},{16,48},{48,16},{1,33},{33,1},{17,49},{49,17},{2,34}... | collective-permute-start | bytes 3145736 | tf_op jit(solution)/shard_map/ppermute | solution.py:22
  60.5 44.2 %collective-permute-done.2 = f32[256,2,512]{2,0,1:T(8,128)S(1)} collective-permute-done((f32[256,2,512]{2,0,1:T(8,128)S(1)}, f32[256,2,512]{2,0,1:T(8,128)S(1)}, u32[]{:S(2)}, u32[]{:S(2)}) %collective-permute-start.2) | collective-permute-done | bytes 1048608 | tf_op jit(solution)/shard_map/ppermute | solution.py:22
  105.7 2.5 collective-permute-done.3
  109.2 45.3 %collective-permute-done.4 = f32[256,2,512]{2,0,1:T(8,128)S(1)} collective-permute-done((f32[256,2,512]{2,0,1:T(8,128)S(1)}, f32[256,2,512]{2,0,1:T(8,128)S(1)}, u32[]{:S(2)}, u32[]{:S(2)}) %collective-permute-start.4) | collective-permute-done | bytes 1048608 | tf_op jit(solution)/shard_map/ppermute | solution.py:22
  155.2 2.8 collective-permute-start.5
  158.2 22.7 %collective-permute-done.5 = f32[256,2,512]{2,0,1:T(8,128)S(1)} collective-permute-done((f32[256,2,512]{2,0,1:T(8,128)S(1)}, f32[256,2,512]{2,0,1:T(8,128)S(1)}, u32[]{:S(2)}, u32[]{:S(2)}) %collective-permute-start.5) | collective-permute-done | bytes 1048608 | tf_op jit(solution)/shard_map/ppermute | solution.py:22
  181.6 3.1 collective-permute-start.6
  184.9 22.4 %collective-permute-done.6 = f32[256,2,512]{2,0,1:T(8,128)S(1)} collective-permute-done((f32[256,2,512]{2,0,1:T(8,128)S(1)}, f32[256,2,512]{2,0,1:T(8,128)S(1)}, u32[]{:S(2)}, u32[]{:S(2)}) %collective-permute-start.6) | collective-permute-done | bytes 1048608 | tf_op jit(solution)/shard_map/ppermute | solution.py:22
  208.0 1.8 collective-permute-start.7
  209.8 21.7 %collective-permute-done.7 = f32[256,2,512]{2,0,1:T(8,128)S(1)} collective-permute-done((f32[256,2,512]{2,0,1:T(8,128)S(1)}, f32[256,2,512]{2,0,1:T(8,128)S(1)}, u32[]{:S(2)}, u32[]{:S(2)}) %collective-permute-start.7) | collective-permute-done | bytes 1048608 | tf_op jit(solution)/shard_map/ppermute | solution.py:22
  232.4 2.0 fusion.4
  234.4 2.0 fusion.5
  236.9 5.2 %rev.3 = f32[256,2,512]{2,0,1:T(8,128)} reverse(f32[256,2,512]{2,0,1:T(8,128)S(1)} %pad_maximum_fusion), dimensions={0} | reverse | bytes 2097152 | tf_op jit(solution)/shard_map/rev | solution.py:114
  242.1 5.5 %slice.131 = f32[255,2,512]{2,0,1:T(8,128)} reverse(f32[255,2,512]{2,0,1:T(8,128)S(1)} %fusion.2), dimensions={0} | reverse | bytes 2088960 | tf_op jit(solution)/shard_map/jit(_roll_static)/slice | solution.py:115
  247.6 1.5 maximum_select_fusion.8
  250.2 9.4 %all-to-all-start.2 = ((f32[16,16,1,2,512]{4,1,3,2,0:T(8,128)}), f32[16,16,1,2,512]{4,1,3,2,0:T(8,128)S(1)}, u32[]{:S(2)}, u32[]{:S(2)}) async-start(f32[16,16,1,2,512]{4,1,3,2,0:T(8,128)} %copy.30), calls=%async_computation.2 | async-start | bytes 2097152 | tf_op jit(solution)/shard_map/all_to_all | solution.py:131
  260.6 30.5 %all-to-all-done.2 = f32[16,16,1,2,512]{4,1,3,2,0:T(8,128)S(1)} async-done(((f32[16,16,1,2,512]{4,1,3,2,0:T(8,128)}), f32[16,16,1,2,512]{4,1,3,2,0:T(8,128)S(1)}, u32[]{:S(2)}, u32[]{:S(2)}) %all-to-all-start.2) | async-done | bytes 1048608 | tf_op jit(solution)/shard_map/all_to_all | solution.py:131
  291.2 3.7 all-to-all-start
  294.9 1.6 copy.31
  296.4 22.1 %all-to-all-done = f32[16,16,1,2,512]{4,1,3,2,0:T(8,128)S(1)} async-done(((f32[16,16,1,2,512]{4,1,3,2,0:T(8,128)}), f32[16,16,1,2,512]{4,1,3,2,0:T(8,128)S(1)}, u32[]{:S(2)}, u32[]{:S(2)}) %all-to-all-start) | async-done | bytes 1048608 | tf_op jit(solution)/shard_map/all_to_all | solution.py:122
  318.5 13.9 %all-to-all-start.3 = ((f32[16,16,1,2,512]{4,0,3,2,1:T(8,128)}), f32[16,16,1,2,512]{4,0,3,2,1:T(8,128)S(1)}, u32[]{:S(2)}, u32[]{:S(2)}) async-start(f32[16,16,1,2,512]{4,0,3,2,1:T(8,128)} %copy.31), calls=%async_computation.3 | async-start | bytes 2097152 | tf_op jit(solution)/shard_map/all_to_all | solution.py:130
  332.4 1.6 copy.28
  334.0 24.1 %all-to-all-done.3 = f32[16,16,1,2,512]{4,0,3,2,1:T(8,128)S(1)} async-done(((f32[16,16,1,2,512]{4,0,3,2,1:T(8,128)}), f32[16,16,1,2,512]{4,0,3,2,1:T(8,128)S(1)}, u32[]{:S(2)}, u32[]{:S(2)}) %all-to-all-start.3) | async-done | bytes 1048608 | tf_op jit(solution)/shard_map/all_to_all | solution.py:130
  358.2 5.1 %all-to-all-start.1 = ((f32[16,16,1,2,512]{4,0,3,2,1:T(8,128)}), f32[16,16,1,2,512]{4,0,3,2,1:T(8,128)S(1)}, u32[]{:S(2)}, u32[]{:S(2)}) async-start(f32[16,16,1,2,512]{4,0,3,2,1:T(8,128)} %copy.28), calls=%async_computation.1 | async-start | bytes 2097152 | tf_op jit(solution)/shard_map/all_to_all | solution.py:121
  365.5 2.7 gather_fusion
  369.6 18.5 %all-to-all-done.1 = f32[16,16,1,2,512]{4,0,3,2,1:T(8,128)S(1)} async-done(((f32[16,16,1,2,512]{4,0,3,2,1:T(8,128)}), f32[16,16,1,2,512]{4,0,3,2,1:T(8,128)S(1)}, u32[]{:S(2)}, u32[]{:S(2)}) %all-to-all-start.1) | async-done | bytes 1048608 | tf_op jit(solution)/shard_map/all_to_all | solution.py:121
  391.2 2.0 fusion.1
  (51 shorter events, 17.2 us)
Async XLA Ops:
  2.7 26.5 %collective-permute-start = (f32[256,2,512]{2,0,1:T(8,128)S(1)}, f32[256,2,512]{2,0,1:T(8,128)S(1)}, u32[]{:S(2)}, u32[]{:S(2)}) collective-permute-start(f32[256,2,512]{2,0,1:T(8,128)S(1)} %copy.23), channel_id=1, source_target_pairs={{0,128},{128,0},{64,192},{192,64},{1,129},{129,1},{65,193},{193,65... | collective-permute-start | bytes 3145736 | tf_op jit(solution)/shard_map/ppermute | solution.py:22
  30.0 24.1 %collective-permute-start.1 = (f32[256,2,512]{2,0,1:T(8,128)S(1)}, f32[256,2,512]{2,0,1:T(8,128)S(1)}, u32[]{:S(2)}, u32[]{:S(2)}) collective-permute-start(f32[256,2,512]{2,0,1:T(8,128)S(1)} %maximum_select_fusion), channel_id=1, source_target_pairs={{0,64},{64,0},{128,192},{192,128},{1,65},{65,1},{129,193},{193,129... | collective-permute-start | bytes 3145736 | tf_op jit(solution)/shard_map/ppermute | solution.py:22
  54.9 49.9 %collective-permute-start.2 = (f32[256,2,512]{2,0,1:T(8,128)S(1)}, f32[256,2,512]{2,0,1:T(8,128)S(1)}, u32[]{:S(2)}, u32[]{:S(2)}) collective-permute-start(f32[256,2,512]{2,0,1:T(8,128)S(1)} %maximum_select_fusion.1), channel_id=1, source_target_pairs={{0,32},{32,0},{16,48},{48,16},{1,33},{33,1},{17,49},{49,17},{2,34}... | collective-permute-start | bytes 3145736 | tf_op jit(solution)/shard_map/ppermute | solution.py:22
  105.4 2.7 collective-permute-start.3
  108.9 45.6 %collective-permute-start.4 = (f32[256,2,512]{2,0,1:T(8,128)S(1)}, f32[256,2,512]{2,0,1:T(8,128)S(1)}, u32[]{:S(2)}, u32[]{:S(2)}) collective-permute-start(f32[256,2,512]{2,0,1:T(8,128)S(1)} %maximum_select_fusion.3), channel_id=1, source_target_pairs={{0,8},{8,0},{1,9},{9,1},{2,10},{10,2},{3,11},{11,3},{4,12},{12,4},... | collective-permute-start | bytes 3145736 | tf_op jit(solution)/shard_map/ppermute | solution.py:22
  155.2 25.7 %collective-permute-start.5 = (f32[256,2,512]{2,0,1:T(8,128)S(1)}, f32[256,2,512]{2,0,1:T(8,128)S(1)}, u32[]{:S(2)}, u32[]{:S(2)}) collective-permute-start(f32[256,2,512]{2,0,1:T(8,128)S(1)} %maximum_select_fusion.4), channel_id=1, source_target_pairs={{0,4},{4,0},{1,5},{5,1},{2,6},{6,2},{3,7},{7,3},{8,12},{12,8},{9,1... | collective-permute-start | bytes 3145736 | tf_op jit(solution)/shard_map/ppermute | solution.py:22
  181.6 25.6 %collective-permute-start.6 = (f32[256,2,512]{2,0,1:T(8,128)S(1)}, f32[256,2,512]{2,0,1:T(8,128)S(1)}, u32[]{:S(2)}, u32[]{:S(2)}) collective-permute-start(f32[256,2,512]{2,0,1:T(8,128)S(1)} %maximum_select_fusion.5), channel_id=1, source_target_pairs={{0,2},{2,0},{1,3},{3,1},{4,6},{6,4},{5,7},{7,5},{8,10},{10,8},{9,1... | collective-permute-start | bytes 3145736 | tf_op jit(solution)/shard_map/ppermute | solution.py:22
  208.0 23.5 %collective-permute-start.7 = (f32[256,2,512]{2,0,1:T(8,128)S(1)}, f32[256,2,512]{2,0,1:T(8,128)S(1)}, u32[]{:S(2)}, u32[]{:S(2)}) collective-permute-start(f32[256,2,512]{2,0,1:T(8,128)S(1)} %maximum_select_fusion.6), channel_id=1, source_target_pairs={{0,1},{1,0},{2,3},{3,2},{4,5},{5,4},{6,7},{7,6},{8,9},{9,8},{10,11... | collective-permute-start | bytes 3145736 | tf_op jit(solution)/shard_map/ppermute | solution.py:22
  242.1 5.5 %copy-start = (f32[256,2,512]{2,0,1:T(8,128)S(1)}, f32[256,2,512]{2,0,1:T(8,128)}, u32[]{:S(2)}) copy-start(f32[256,2,512]{2,0,1:T(8,128)} %rev.3) | copy-start | bytes 3145732
  250.2 41.0 %all-to-all-start.2 = ((f32[16,16,1,2,512]{4,1,3,2,0:T(8,128)}), f32[16,16,1,2,512]{4,1,3,2,0:T(8,128)S(1)}, u32[]{:S(2)}, u32[]{:S(2)}) async-start(f32[16,16,1,2,512]{4,1,3,2,0:T(8,128)} %copy.30), calls=%async_computation.2 | async-start | bytes 2097152 | tf_op jit(solution)/shard_map/all_to_all | solution.py:131
  291.2 27.3 %all-to-all-start = ((f32[16,16,1,2,512]{4,1,3,2,0:T(8,128)}), f32[16,16,1,2,512]{4,1,3,2,0:T(8,128)S(1)}, u32[]{:S(2)}, u32[]{:S(2)}) async-start(f32[16,16,1,2,512]{4,1,3,2,0:T(8,128)} %pad_maximum_fusion.2), calls=%async_computation | async-start | bytes 2097152 | tf_op jit(solution)/shard_map/all_to_all | solution.py:122
  318.5 39.7 %all-to-all-start.3 = ((f32[16,16,1,2,512]{4,0,3,2,1:T(8,128)}), f32[16,16,1,2,512]{4,0,3,2,1:T(8,128)S(1)}, u32[]{:S(2)}, u32[]{:S(2)}) async-start(f32[16,16,1,2,512]{4,0,3,2,1:T(8,128)} %copy.31), calls=%async_computation.3 | async-start | bytes 2097152 | tf_op jit(solution)/shard_map/all_to_all | solution.py:130
  358.2 29.9 %all-to-all-start.1 = ((f32[16,16,1,2,512]{4,0,3,2,1:T(8,128)}), f32[16,16,1,2,512]{4,0,3,2,1:T(8,128)S(1)}, u32[]{:S(2)}, u32[]{:S(2)}) async-start(f32[16,16,1,2,512]{4,0,3,2,1:T(8,128)} %copy.28), calls=%async_computation.1 | async-start | bytes 2097152 | tf_op jit(solution)/shard_map/all_to_all | solution.py:121
  363.3 0.7 copy-start.1
  364.0 0.7 copy-start.2
where the time goes:
time: 396 us; the launch traced here: 395 us
  waiting for transfers between devices  299 us (76%)
  starting transfers between devices  50.4 us (13%)
  local copies, waits for them, and re-layouts  24.2 us (6%)
  other arithmetic  10.6 us (3%)
  matrix products  8.18 us (2%)
    ppermute x8, waiting for transfers between devices, swapped(): return lax.ppermute(block, axis, route)  204 us
    all_to_all x1, waiting for transfers between devices, by_sections(): lax.all_to_all(mirrored.reshape(shape_out), ('gx', 'gy'), split_axis=0, c...  30.5 us
    all_to_all x1, waiting for transfers between devices, by_sections(): lax.all_to_all(lax.all_to_all(mirrored.reshape(shape_out), ('gx', 'gy'),...  24.1 us
    all_to_all x1, waiting for transfers between devices, by_sections(): lax.all_to_all(spectrum.reshape(shape_out), ('gx', 'gy'), split_axis=0, c...  22.1 us
    all_to_all x1, waiting for transfers between devices, by_sections(): lax.all_to_all(lax.all_to_all(spectrum.reshape(shape_out), ('gx', 'gy'),...  18.5 us
    ppermute x8, starting transfers between devices, swapped(): return lax.ppermute(block, axis, route)  18.3 us
    all_to_all x1, starting transfers between devices, by_sections(): lax.all_to_all(lax.all_to_all(mirrored.reshape(shape_out), ('gx', 'gy'),...  13.9 us
    all_to_all x1, starting transfers between devices, by_sections(): lax.all_to_all(mirrored.reshape(shape_out), ('gx', 'gy'), split_axis=0, c...  9.44 us
  transfers between devices with their start and end apart: 12, of which 12 were waited for; matrix products, arithmetic and copies ran while one was open for 2% of the time, Pallas kernels for 0%

commit v1 on v0

v1 whole, which is shorter than its diff:
```python
import jax
import jax.numpy as jnp
import numpy as np
from jax import lax
from jax.experimental import pallas as pl
from jax.experimental.pallas import tpu as pltpu
from jax.sharding import PartitionSpec as P

MESH = pl.DeviceIdType.MESH
AXES = ("gx", "gy", "gz")
STEPS = 131072
F32, BF16 = jnp.float32, jnp.bfloat16
Z_ORDER = [(d * s, c) for d in (1, 2, 3) for c in (0, 1) for s in (1, -1)] + [(4, 0), (4, 1), (0, 1)]
XY_ORDER = [
    (1, 0), (-1, 0), (0, 1), (0, -1), (1, 1), (-1, -1), (1, -1), (-1, 1),
    (2, 1), (1, 2), (2, -1), (-1, 2), (2, 0), (0, 2), (2, 2),
]


def halves(table):
    high = np.asarray(table, np.float32).astype(jnp.bfloat16)
    low = (np.asarray(table, np.float32) - high.astype(np.float32)).astype(jnp.bfloat16)
    return np.stack([high, low])


def tables():
    position = np.arange(256)
    xy, zc = position // 16, position % 16
    x, y = xy // 8 + 2 * (xy // 4 % 2), xy % 4
    z, core = zc // 2, zc % 2
    device = y * 64 + z // 4 * 32 + core * 16 + z % 4 * 4 + x
    r = np.arange(128)
    turn = 2.0 * np.pi / 256
    first = np.concatenate(
        [
            np.cos(turn * (np.outer(r, device) % 256)),
            np.cos(turn * (128 * device % 256))[None],
            -np.sin(turn * (np.outer(r[1:], device) % 256)),
        ]
    )
    m = np.arange(512)
    twist = 2.0 * np.pi / STEPS * np.outer(np.arange(136), m)
    valid = (np.arange(136) <= 128)[:, None]
    twiddle = np.stack([np.cos(twist) * valid, np.sin(twist) * valid]).astype(np.float32)
    even, odd = device[:128], device[128:]
    m = np.arange(256)
    angle_e = 2.0 * np.pi / 512 * (np.outer(np.concatenate([even, 511 - odd]), m) % 512)
    angle_o = 2.0 * np.pi / 512 * (np.outer(np.concatenate([511 - even, odd]), m) % 512)
    second = np.stack([halves(f(a)) for a in (angle_e, angle_o) for f in (np.cos, np.sin)])
    return halves(first), twiddle, second


def split(value):
    high = value.astype(BF16)
    return high, (value - high.astype(F32)).astype(BF16)


def product(a, b, contract):
    def one(left, right):
        return lax.dot_general(left, right, (contract, ((), ())), preferred_element_type=F32)

    return one(a[0], b[0]) + (one(a[0], b[1]) + one(a[1], b[0]))


def exchange_kernel(
    x_hbm, first_hbm, twiddle_hbm, second_hbm, out,
    x_in, first, twiddle, second, send1, mid1, recv1, send2, mid2,
    load_sem, z_send, z_recv, xy_send, xy_recv, own_sem,
):
    y = lax.axis_index("gx")
    gy, gz = lax.axis_index("gy"), lax.axis_index("gz")
    z_hi, core = gy // 2, gy % 2
    z_lo, x = gz // 4, gz % 4
    z = z_hi * 4 + z_lo
    my_zc = z * 2 + core
    my_xy = x % 2 * 8 + x // 2 * 4 + y
    z_peers, xy_peers = [], []
    for dz, dc in Z_ORDER:
        pz = (z + dz + 8) % 8
        pc = 1 - core if dc else core
        z_peers.append((pz * 2 + pc, (y, pz // 4 * 2 + pc, pz % 4 * 4 + x)))
    for dx, dy in XY_ORDER:
        px, py = (x + dx + 4) % 4, (y + dy + 4) % 4
        xy_peers.append((px % 2 * 8 + px // 2 * 4 + py, (py, gy, z_lo * 4 + px)))

    load_x = pltpu.make_async_copy(x_hbm, x_in, load_sem.at[0])
    load_x.start()
    barrier = pltpu.get_barrier_semaphore()
    for _, peer in z_peers + xy_peers:
        pl.semaphore_signal(barrier, inc=1, device_id=peer, device_id_type=MESH)
    loads = [
        pltpu.make_async_copy(source, target, load_sem.at[1 + i])
        for i, (source, target) in enumerate(((first_hbm, first), (twiddle_hbm, twiddle), (second_hbm, second)))
    ]
    for load in loads:
        load.start()

    def over_z(source, target, stage, h, target_outer):
        k = stage * 2 + h
        def place(ref):
            return ref.at[h, my_zc] if target_outer else ref.at[h, :, my_zc]
        for zc, peer in z_peers:
            pltpu.make_async_remote_copy(
                src_ref=source.at[h, :, zc], dst_ref=place(target), send_sem=z_send.at[k], recv_sem=z_recv.at[k],
                device_id=peer, device_id_type=MESH,
            ).start()
        pltpu.make_async_copy(source.at[h, :, my_zc], place(target), own_sem.at[k]).start()

    def over_xy(source, target, stage, h, source_outer):
        k = stage * 2 + h
        def piece(xy):
            return source.at[h, xy] if source_outer else source.at[h, :, xy]
        for xy, peer in xy_peers:
            pltpu.make_async_remote_copy(
                src_ref=piece(xy), dst_ref=target.at[h, my_xy], send_sem=xy_send.at[k], recv_sem=xy_recv.at[k],
                device_id=peer, device_id_type=MESH,
            ).start()
        pltpu.make_async_copy(piece(my_xy), target.at[h, my_xy], own_sem.at[4 + k]).start()

    def wait(target, stage, h, is_z):
        k = stage * 2 + h
        send, recv = (z_send, z_recv) if is_z else (xy_send, xy_recv)
        some = target.at[h, pl.ds(0, 15)]
        pltpu.make_async_copy(some, some, recv.at[k]).wait()
        pltpu.make_async_copy(some, some, send.at[k]).wait()
        one = target.at[h, 0]
        pltpu.make_async_copy(one, one, own_sem.at[k if is_z else 4 + k]).wait()

    flat1 = send1.reshape(2048, 128)
    load_x.wait()
    for h in range(2):
        for k in (2 * h, 2 * h + 1):
            for q in range(4):
                turned = x_in[pl.ds(128 * q, 128), pl.ds(128 * k, 128)].T
                flat1[pl.ds(512 * k + q, 128, stride=4), :] = turned
    pl.semaphore_wait(barrier, 30)

    over_z(send1, mid1, 0, 0, True)
    over_xy(send1, mid1, 0, 1, True)
    for load in loads:
        load.wait()

    def transform(h):
        received = recv1.reshape(2048, 128)
        cos_sin = []
        for side in range(2):
            rows = jnp.concatenate(
                [received[pl.ds(1024 * h + 2 * side + q, 256, stride=4), :] for q in range(2)], axis=1
            )
            mixed = product((first[0], first[1]), split(rows), ((1,), (0,)))
            lanes = pl.ds(256 * side, 256)
            cosine, sine = twiddle[0, :, lanes], twiddle[1, :, lanes]
            re, im = mixed[:128], mixed[128:]
            z_re = re * cosine[:128] + im * sine[:128]
            z_im = im * cosine[:128] - re * sine[:128]
            row = lax.broadcasted_iota(jnp.int32, (128, 256), 0)
            z_im = jnp.where(row == 0, 0.0, z_im)
            h_re = im[:8] * cosine[128:]
            h_im = -im[:8] * sine[128:]
            cos_sin.append((z_re, z_im, h_re, h_im))
        flat2 = send2.reshape(2048, 128)
        lane = lax.broadcasted_iota(jnp.int32, (128, 128), 1)
        for parity in range(2):
            if parity == 0:
                z_re, z_im, h_re, h_im = (a + b for a, b in zip(*cos_sin))
            else:
                z_re, z_im, h_re, h_im = (a - b for a, b in zip(*cos_sin))
            right = split(jnp.concatenate([z_re, z_im], axis=0))
            cosine = (second[2 * parity, 0], second[2 * parity, 1])
            sine = (second[2 * parity + 1, 0], second[2 * parity + 1, 1])
            nt = ((1,), (1,))
            by_cos = product(cosine, right, nt)
            by_sin = product(sine, right, nt)
            out_re = by_cos[:, :128] + by_sin[:, 128:]
            out_im = by_cos[:, 128:] - by_sin[:, :128]
            straight = slice(0, 128) if parity == 0 else slice(128, 256)
            mirror = slice(128, 256) if parity == 0 else slice(0, 128)
            middle_c = split(jnp.concatenate([h_re[:1], h_im[:1], jnp.zeros((126, 256), F32)], axis=0))
            middle_s = split(jnp.concatenate([h_im[:1], -h_re[:1], jnp.zeros((126, 256), F32)], axis=0))
            middle = product(tuple(c[straight] for c in cosine), middle_c, nt)
            middle = middle + product(tuple(s[straight] for s in sine), middle_s, nt)
            base = 1024 * h + 512 * parity
            flat2[pl.ds(base + 0, 128, stride=4), :] = out_re[straight]
            flat2[pl.ds(base + 2, 128, stride=4), :] = out_im[straight]
            mids[parity] = middle
            other = 1024 * h + 512 * (1 - parity)
            mirrors[1 - parity] = (out_re[mirror], -out_im[mirror])
            del other
        for parity in range(2):
            base = 1024 * h + 512 * parity
            m_re, m_im = mirrors[parity]
            middle = mids[parity]
            flat2[pl.ds(base + 1, 128, stride=4), :] = jnp.where(lane == 0, middle, m_re)
            flat2[pl.ds(base + 3, 128, stride=4), :] = jnp.where(lane == 0, pltpu.roll(middle, 127, 1), m_im)

    mids, mirrors = {}, {}

    wait(mid1, 0, 1, False)
    over_z(mid1, recv1, 0, 1, False)
    wait(mid1, 0, 0, True)
    over_xy(mid1, recv1, 0, 0, False)
    wait(recv1, 0, 0, False)
    transform(0)
    over_z(send2, mid2, 1, 0, True)
    wait(recv1, 0, 1, True)
    transform(1)
    over_xy(send2, mid2, 1, 1, True)
    wait(mid2, 1, 1, False)
    over_z(mid2, out, 1, 1, False)
    wait(mid2, 1, 0, True)
    over_xy(mid2, out, 1, 0, False)
    wait(out, 1, 0, False)
    wait(out, 1, 1, True)


def exchange(currents):
    first, twiddle, second = tables()
    buffer = pltpu.VMEM((2, 16, 16, 4, 128), F32)
    anywhere = pl.BlockSpec(memory_space=pl.ANY)
    dma = pltpu.SemaphoreType.DMA
    return pl.pallas_call(
        exchange_kernel,
        out_shape=jax.ShapeDtypeStruct((2, 16, 16, 4, 128), F32),
        in_specs=[anywhere] * 4,
        out_specs=pl.BlockSpec(memory_space=pltpu.VMEM),
        scratch_shapes=[
            pltpu.VMEM((512, 512), F32),
            pltpu.VMEM(first.shape, BF16),
            pltpu.VMEM(twiddle.shape, F32),
            pltpu.VMEM(second.shape, BF16),
            buffer, buffer, buffer, buffer, buffer,
            dma((4,)), dma((4,)), dma((4,)), dma((4,)), dma((4,)), dma((8,)),
        ],
        compiler_params=pltpu.CompilerParams(collective_id=0, has_side_effects=True, vmem_limit_bytes=48 * 1024 * 1024),
        name="exchange",
    )(currents, first, twiddle, second)


def gram_kernel(v, power, cross, high, low, turned_high, turned_low):
    step = pl.program_id(0)

    @pl.when(step == 0)
    def _():
        rows = v.reshape(2048, 128)
        for q in range(4):
            part = rows[pl.ds(q, 512, stride=4), :]
            top, rest = split(part)
            high[:, 128 * q:128 * q + 128] = top
            low[:, 128 * q:128 * q + 128] = rest
            place = 128 * ((q + 2) % 4)
            sign = 1.0 if q >= 2 else -1.0
            turned_high[:, place:place + 128] = (top.astype(F32) * sign).astype(BF16)
            turned_low[:, place:place + 128] = (rest.astype(F32) * sign).astype(BF16)

    nt = ((1,), (1,))
    size = power.shape[0]
    here = pl.ds(pl.multiple_of(step * size, size), size)
    right = (high[...], low[...])
    scaling = 1.0 / (float(STEPS) * 256.0)
    power[...] = product((high[here, :], low[here, :]), right, nt) * scaling
    cross[...] = product((turned_high[here, :], turned_low[here, :]), right, nt) * scaling


def gram(v):
    block = pl.BlockSpec((None, 128, 512), lambda i: (0, i, 0))
    shape = jax.ShapeDtypeStruct((1, 512, 512), F32)
    return pl.pallas_call(
        gram_kernel,
        grid=(4,),
        out_shape=(shape, shape),
        in_specs=[pl.BlockSpec((512, 4, 128), lambda i: (0, 0, 0), pipeline_mode=pl.Buffered(1))],
        out_specs=(block, block),
        scratch_shapes=[pltpu.VMEM((512, 512), BF16)] * 4,
        name="gram",
    )(v)


def on_device(currents):
    return gram(exchange(currents).reshape(512, 4, 128))


def solution(mesh):
    spec = P(AXES, None, None)
    return jax.shard_map(
        on_device, mesh=mesh, in_specs=(P(AXES, None),), out_specs=(spec, spec), check_vma=False
    )
```

time: 396 us -> 74.9 us (0.19)
  waiting for transfers between devices: 299 us -> 0 us
  Pallas kernels: 0 us -> 67.4 us
  starting transfers between devices: 50.4 us -> 0 us
  local copies, waits for them, and re-layouts: 24.2 us -> 5.4 us
  other arithmetic: 10.6 us -> 0 us
  matrix products: 8.18 us -> 0 us
    ppermute x8 -> x0, waiting for transfers between devices: 204 us -> none  [swapped(): return lax.ppermute(block, axis, route)]
    all_to_all x4 -> x0, waiting for transfers between devices: 95.2 us -> none  [the longest x1 30.5 us: by_sections(): lax.all_to_all(mirrored.reshape(shape_out), ('gx', 'gy'), split_axis=0, c...]
    pallas_call x0 -> x2, Pallas kernels: none -> 67.4 us  [the longest x1 60.5 us: exchange(): pl.pallas_call(exchange_kernel, out_shape=jax.ShapeDtypeStruct((2, 16, 16...]
    all_to_all x4 -> x0, starting transfers between devices: 32.2 us -> none  [the longest x1 13.9 us: by_sections(): lax.all_to_all(lax.all_to_all(mirrored.reshape(shape_out), ('gx', 'gy'),...]
    ppermute x8 -> x0, starting transfers between devices: 18.3 us -> none  [swapped(): return lax.ppermute(block, axis, route)]
    dot_general x5 -> x0, matrix products: 8.18 us -> none  [the longest x1 2.03 us: by_sections(): with_sin = jnp.einsum('jm,mkn->jkn', sin_table, stacked, precision=PRECISE)]
    slice x1 -> x0, local copies, waits for them, and re-layouts: 5.54 us -> none  [by_sections(): jnp.roll(reversed_rows, 1, axis=0)]
    rev x1 -> x0, local copies, waits for them, and re-layouts: 5.2 us -> none  [by_sections(): reversed_rows = spectrum[::-1]]
  transfers between devices with their start and end apart: 12 -> 0, of which waited for: 12 -> 0; matrix products, arithmetic and copies ran while one was open for 2% -> 0% of each run, Pallas kernels for 0% -> 0%
where the time goes in v1:
time: 74.9 us; the launch traced here: 73.5 us
  Pallas kernels  67.4 us (90%)
  local copies, waits for them, and re-layouts  5.4 us (7%)
    pallas_call x1, Pallas kernels, exchange(): pl.pallas_call(exchange_kernel, out_shape=jax.ShapeDtypeStruct((2, 16, 16...  60.5 us
    pallas_call x1, Pallas kernels, gram(): pl.pallas_call(gram_kernel, grid=(4,), out_shape=(shape, shape), in_specs...  6.94 us
    unnamed x10, local copies, waits for them, and re-layouts  5.4 us

profile of v1, /device:TPU:64, one launch (start us, length us, event | category | flops | bytes accessed | tf_op | source)
XLA Modules:
  0.0 73.5 jit_solution(4146550675414634179)
XLA Ops:
  0.6 0.0 copy-start.1
  0.6 1.2 %copy-done.1 = f32[512,512]{1,0:T(8,128)S(1)} copy-done((f32[512,512]{1,0:T(8,128)S(1)}, f32[512,512]{1,0:T(8,128)}, u32[]{:S(2)}) %copy-start.1) | copy-done | bytes 1048600
  1.9 0.0 copy-start.2
  1.9 1.2 %copy-done.2 = bf16[4,2,256,256]{3,2,1,0:T(8,128)(2,1)S(1)} copy-done((bf16[4,2,256,256]{3,2,1,0:T(8,128)(2,1)S(1)}, bf16[4,2,256,256]{3,2,1,0:T(8,128)(2,1)}, u32[]{:S(2)}) %copy-start.2) | copy-done | bytes 1048600
  3.1 0.0 copy-start.3
  3.1 1.1 %copy-done.3 = f32[2,136,512]{2,1,0:T(8,128)S(1)} copy-done((f32[2,136,512]{2,1,0:T(8,128)S(1)}, f32[2,136,512]{2,1,0:T(8,128)}, u32[]{:S(2)}) %copy-start.3) | copy-done | bytes 557080
  4.1 0.0 copy-start.4
  4.1 0.9 %copy-done.4 = bf16[2,256,256]{2,1,0:T(8,128)(2,1)S(1)} copy-done((bf16[2,256,256]{2,1,0:T(8,128)(2,1)S(1)}, bf16[2,256,256]{2,1,0:T(8,128)(2,1)}, u32[]{:S(2)}) %copy-start.4) | copy-done | bytes 262168
  5.1 60.5 %exchange.1 = f32[2,16,16,4,128]{4,3,2,1,0:T(4,128)S(1)} custom-call(f32[512,512]{1,0:T(8,128)S(1)} %copy-done.1, bf16[2,256,256]{2,1,0:T(8,128)(2,1)S(1)} %copy-done.4, f32[2,136,512]{2,1,0:T(8,128)S(1)} %copy-done.3, bf16[4,2,256,256]{3,2,1,0:T(8,128)(2,1)S(1)} %copy-done.2), custom_call_target="tpu_custom_call" | custom-call | tf_op jit(solution)/shard_map/exchange/pallas_call | solution.py:221
  65.6 0.0 copy-start
  65.6 1.0 %copy-done = f32[2,16,16,4,128]{4,3,2,1,0:T(4,128)} copy-done((f32[2,16,16,4,128]{4,3,2,1,0:T(4,128)}, f32[2,16,16,4,128]{4,3,2,1,0:T(4,128)S(1)}, u32[]{:S(2)}) %copy-start) | copy-done | bytes 1048600
  66.6 6.9 %gram.1 = (f32[1,512,512]{2,1,0:T(8,128)}, f32[1,512,512]{2,1,0:T(8,128)}) custom-call(f32[512,4,128]{2,1,0:T(4,128)} %bitcast.1), custom_call_target="tpu_custom_call" | custom-call | tf_op jit(solution)/shard_map/gram/pallas_call | solution.py:267
Async XLA Ops:
  0.6 1.2 %copy-start.1 = (f32[512,512]{1,0:T(8,128)S(1)}, f32[512,512]{1,0:T(8,128)}, u32[]{:S(2)}) copy-start(f32[512,512]{1,0:T(8,128)} %x_hbm.1) | copy-start | bytes 3145732
  1.9 1.2 %copy-start.2 = (bf16[4,2,256,256]{3,2,1,0:T(8,128)(2,1)S(1)}, bf16[4,2,256,256]{3,2,1,0:T(8,128)(2,1)}, u32[]{:S(2)}) copy-start(bf16[4,2,256,256]{3,2,1,0:T(8,128)(2,1)} %constant.8.clone.second_hbm) | copy-start | bytes 3145732
  3.1 1.1 %copy-start.3 = (f32[2,136,512]{2,1,0:T(8,128)S(1)}, f32[2,136,512]{2,1,0:T(8,128)}, u32[]{:S(2)}) copy-start(f32[2,136,512]{2,1,0:T(8,128)} %constant.7.clone.twiddle_hbm) | copy-start | bytes 1671172
  4.1 0.9 %copy-start.4 = (bf16[2,256,256]{2,1,0:T(8,128)(2,1)S(1)}, bf16[2,256,256]{2,1,0:T(8,128)(2,1)}, u32[]{:S(2)}) copy-start(bf16[2,256,256]{2,1,0:T(8,128)(2,1)} %constant.6.clone.first_hbm) | copy-start | bytes 786436
  65.6 1.0 %copy-start = (f32[2,16,16,4,128]{4,3,2,1,0:T(4,128)}, f32[2,16,16,4,128]{4,3,2,1,0:T(4,128)S(1)}, u32[]{:S(2)}) copy-start(f32[2,16,16,4,128]{4,3,2,1,0:T(4,128)S(1)} %exchange.1) | copy-start | bytes 3145732

commit v2 on v1

--- a/solution.py
+++ b/solution.py
@@ -15,12 +15,6 @@
     (1, 0), (-1, 0), (0, 1), (0, -1), (1, 1), (-1, -1), (1, -1), (-1, 1),
     (2, 1), (1, 2), (2, -1), (-1, 2), (2, 0), (0, 2), (2, 2),
 ]
-
-
-def halves(table):
-    high = np.asarray(table, np.float32).astype(jnp.bfloat16)
-    low = (np.asarray(table, np.float32) - high.astype(np.float32)).astype(jnp.bfloat16)
-    return np.stack([high, low])
 
 
 def tables():
@@ -41,13 +35,14 @@
     m = np.arange(512)
     twist = 2.0 * np.pi / STEPS * np.outer(np.arange(136), m)
     valid = (np.arange(136) <= 128)[:, None]
-    twiddle = np.stack([np.cos(twist) * valid, np.sin(twist) * valid]).astype(np.float32)
+    twiddle = np.stack([np.cos(twist) * valid, np.sin(twist) * valid])
+    twiddle = twiddle.reshape(2, 136, 2, 256).transpose(0, 2, 1, 3).reshape(544, 256)
     even, odd = device[:128], device[128:]
     m = np.arange(256)
     angle_e = 2.0 * np.pi / 512 * (np.outer(np.concatenate([even, 511 - odd]), m) % 512)
     angle_o = 2.0 * np.pi / 512 * (np.outer(np.concatenate([511 - even, odd]), m) % 512)
-    second = np.stack([halves(f(a)) for a in (angle_e, angle_o) for f in (np.cos, np.sin)])
-    return halves(first), twiddle, second
+    second = [f(angle) for angle in (angle_e, angle_o) for f in (np.cos, np.sin)]
+    return np.concatenate([first, *second, twiddle]).astype(np.float32)
 
 
 def split(value):
@@ -63,8 +58,8 @@
 
 
 def exchange_kernel(
-    x_hbm, first_hbm, twiddle_hbm, second_hbm, out,
-    x_in, first, twiddle, second, send1, mid1, recv1, send2, mid2,
+    x_hbm, table_hbm, power, cross,
+    x_in, table, high, low, send1, mid1, recv1, send2, mid2, out, plain, turned_w,
     load_sem, z_send, z_recv, xy_send, xy_recv, own_sem,
 ):
     y = lax.axis_index("gx")
@@ -88,12 +83,8 @@
     barrier = pltpu.get_barrier_semaphore()
     for _, peer in z_peers + xy_peers:
         pl.semaphore_signal(barrier, inc=1, device_id=peer, device_id_type=MESH)
-    loads = [
-        pltpu.make_async_copy(source, target, load_sem.at[1 + i])
-        for i, (source, target) in enumerate(((first_hbm, first), (twiddle_hbm, twiddle), (second_hbm, second)))
-    ]
-    for load in loads:
-        load.start()
+    load_table = pltpu.make_async_copy(table_hbm, table, load_sem.at[1])
+    load_table.start()
 
     def over_z(source, target, stage, h, target_outer):
         k = stage * 2 + h
@@ -137,8 +128,14 @@
 
     over_z(send1, mid1, 0, 0, True)
     over_xy(send1, mid1, 0, 1, True)
-    for load in loads:
-        load.wait()
+    load_table.wait()
+    for i in range(5):
+        rows = pl.ds(256 * i, 256)
+        high[rows, :], low[rows, :] = split(table[rows, :])
+
+    def matrix(i, start=0, size=256):
+        rows = pl.ds(256 * i + start, size)
+        return high[rows, :], low[rows, :]
 
     def transform(h):
         received = recv1.reshape(2048, 128)
@@ -147,9 +144,9 @@
             rows = jnp.concatenate(
                 [received[pl.ds(1024 * h + 2 * side + q, 256, stride=4), :] for q in range(2)], axis=1
             )
-            mixed = product((first[0], first[1]), split(rows), ((1,), (0,)))
-            lanes = pl.ds(256 * side, 256)
-            cosine, sine = twiddle[0, :, lanes], twiddle[1, :, lanes]
+            mixed = product(matrix(0), split(rows), ((1,), (0,)))
+            cosine = table[pl.ds(1280 + 136 * side, 136), :]
+            sine = table[pl.ds(1552 + 136 * side, 136), :]
             re, im = mixed[:128], mixed[128:]
             z_re = re * cosine[:128] + im * sine[:128]
             z_im = im * cosine[:128] - re * sine[:128]
@@ -166,26 +163,22 @@
             else:
                 z_re, z_im, h_re, h_im = (a - b for a, b in zip(*cos_sin))
             right = split(jnp.concatenate([z_re, z_im], axis=0))
-            cosine = (second[2 * parity, 0], second[2 * parity, 1])
-            sine = (second[2 * parity + 1, 0], second[2 * parity + 1, 1])
             nt = ((1,), (1,))
-            by_cos = product(cosine, right, nt)
-            by_sin = product(sine, right, nt)
+            by_cos = product(matrix(1 + 2 * parity), right, nt)
+            by_sin = product(matrix(2 + 2 * parity), right, nt)
             out_re = by_cos[:, :128] + by_sin[:, 128:]
             out_im = by_cos[:, 128:] - by_sin[:, :128]
             straight = slice(0, 128) if parity == 0 else slice(128, 256)
             mirror = slice(128, 256) if parity == 0 else slice(0, 128)
             middle_c = split(jnp.concatenate([h_re[:1], h_im[:1], jnp.zeros((126, 256), F32)], axis=0))
             middle_s = split(jnp.concatenate([h_im[:1], -h_re[:1], jnp.zeros((126, 256), F32)], axis=0))
-            middle = product(tuple(c[straight] for c in cosine), middle_c, nt)
-            middle = middle + product(tuple(s[straight] for s in sine), middle_s, nt)
+            middle = product(matrix(1 + 2 * parity, 128 * parity, 128), middle_c, nt)
+            middle = middle + product(matrix(2 + 2 * parity, 128 * parity, 128), middle_s, nt)
             base = 1024 * h + 512 * parity
             flat2[pl.ds(base + 0, 128, stride=4), :] = out_re[straight]
             flat2[pl.ds(base + 2, 128, stride=4), :] = out_im[straight]
             mids[parity] = middle
-            other = 1024 * h + 512 * (1 - parity)
             mirrors[1 - parity] = (out_re[mirror], -out_im[mirror])
-            del other
         for parity in range(2):
             base = 1024 * h + 512 * parity
             m_re, m_im = mirrors[parity]
@@ -209,74 +202,67 @@
     over_z(mid2, out, 1, 1, False)
     wait(mid2, 1, 0, True)
     over_xy(mid2, out, 1, 0, False)
+    def spread(h):
+        rows = out.reshape(2048, 128)
+        here = pl.ds(256 * h, 256)
+        for q in range(4):
+            high, low = split(rows[pl.ds(1024 * h + q, 256, stride=4), :])
+            place = pl.ds(128 * q, 128)
+            plain[0, here, place] = high
+            plain[1, here, place] = low
+            place = pl.ds(128 * ((q + 2) % 4), 128)
+            turned_w[0, here, place] = high if q >= 2 else -high
+            turned_w[1, here, place] = low if q >= 2 else -low
+
+    nt = ((1,), (1,))
+    scaling = 1.0 / (float(STEPS) * 256.0)
+
+    def block(i, j):
+        a, b = pl.ds(256 * i, 256), pl.ds(256 * j, 256)
+        right = (plain[0, b, :], plain[1, b, :])
+        p = product((plain[0, a, :], plain[1, a, :]), right, nt) * scaling
+        c = product((turned_w[0, a, :], turned_w[1, a, :]), right, nt) * scaling
+        power[0, a, b] = p
+        cross[0, a, b] = c
+        if i != j:
+            power[0, b, a] = p.T
+            cross[0, b, a] = -c.T
+
     wait(out, 1, 0, False)
+    spread(0)
+    block(0, 0)
     wait(out, 1, 1, True)
+    spread(1)
+    block(0, 1)
+    block(1, 1)
 
 
 def exchange(currents):
-    first, twiddle, second = tables()
+    table = tables()
     buffer = pltpu.VMEM((2, 16, 16, 4, 128), F32)
     anywhere = pl.BlockSpec(memory_space=pl.ANY)
     dma = pltpu.SemaphoreType.DMA
     return pl.pallas_call(
         exchange_kernel,
-        out_shape=jax.ShapeDtypeStruct((2, 16, 16, 4, 128), F32),
-        in_specs=[anywhere] * 4,
-        out_specs=pl.BlockSpec(memory_space=pltpu.VMEM),
+        out_shape=(jax.ShapeDtypeStruct((1, 512, 512), F32),) * 2,
+        in_specs=[anywhere] * 2,
+        out_specs=(pl.BlockSpec(memory_space=pltpu.VMEM),) * 2,
         scratch_shapes=[
             pltpu.VMEM((512, 512), F32),
-            pltpu.VMEM(first.shape, BF16),
-            pltpu.VMEM(twiddle.shape, F32),
-            pltpu.VMEM(second.shape, BF16),
-            buffer, buffer, buffer, buffer, buffer,
-            dma((4,)), dma((4,)), dma((4,)), dma((4,)), dma((4,)), dma((8,)),
+            pltpu.VMEM(table.shape, F32),
+            pltpu.VMEM((1280, 256), BF16),
+            pltpu.VMEM((1280, 256), BF16),
+            buffer, buffer, buffer, buffer, buffer, buffer,
+            pltpu.VMEM((2, 512, 512), BF16), pltpu.VMEM((2, 512, 512), BF16),
+            dma((2,)), dma((4,)), dma((4,)), dma((4,)), dma((4,)), dma((8,)),
         ],
-        compiler_params=pltpu.CompilerParams(collective_id=0, has_side_effects=True, vmem_limit_bytes=48 * 1024 * 1024),
+        compiler_params=pltpu.CompilerParams(collective_id=0, has_side_effects=True, vmem_limit_bytes=51 * 1024 * 1024),
         name="exchange",
-    )(currents, first, twiddle, second)
-
-
-def gram_kernel(v, power, cross, high, low, turned_high, turned_low):
-    step = pl.program_id(0)
-
-    @pl.when(step == 0)
-    def _():
-        rows = v.reshape(2048, 128)
-        for q in range(4):
-            part = rows[pl.ds(q, 512, stride=4), :]
-            top, rest = split(part)
-            high[:, 128 * q:128 * q + 128] = top
-            low[:, 128 * q:128 * q + 128] = rest
-            place = 128 * ((q + 2) % 4)
-            sign = 1.0 if q >= 2 else -1.0
-            turned_high[:, place:place + 128] = (top.astype(F32) * sign).astype(BF16)
-            turned_low[:, place:place + 128] = (rest.astype(F32) * sign).astype(BF16)
-
-    nt = ((1,), (1,))
-    size = power.shape[0]
-    here = pl.ds(pl.multiple_of(step * size, size), size)
-    right = (high[...], low[...])
-    scaling = 1.0 / (float(STEPS) * 256.0)
-    power[...] = product((high[here, :], low[here, :]), right, nt) * scaling
-    cross[...] = product((turned_high[here, :], turned_low[here, :]), right, nt) * scaling
-
-
-def gram(v):
-    block = pl.BlockSpec((None, 128, 512), lambda i: (0, i, 0))
-    shape = jax.ShapeDtypeStruct((1, 512, 512), F32)
-    return pl.pallas_call(
-        gram_kernel,
-        grid=(4,),
-        out_shape=(shape, shape),
-        in_specs=[pl.BlockSpec((512, 4, 128), lambda i: (0, 0, 0), pipeline_mode=pl.Buffered(1))],
-        out_specs=(block, block),
-        scratch_shapes=[pltpu.VMEM((512, 512), BF16)] * 4,
-        name="gram",
-    )(v)
+    )(currents, table)
 
 
 def on_device(currents):
-    return gram(exchange(currents).reshape(512, 4, 128))
+    return exchange(currents)
 
 
 def solution(mesh):

time: 74.9 us -> 65.6 us (0.88)
  Pallas kernels: 67.4 us -> 61.8 us
  local copies, waits for them, and re-layouts: 5.4 us -> 1.94 us
    pallas_call x2 -> x1, Pallas kernels: 67.4 us -> 61.8 us  [exchange(): pl.pallas_call(exchange_kernel, out_shape=(jax.ShapeDtypeStruct((1, 512,...]
    unnamed x10 -> x2, local copies, waits for them, and re-layouts: 5.4 us -> 1.94 us
where the time goes in v2:
time: 65.6 us; the launch traced here: 64.4 us
  Pallas kernels  61.8 us (94%)
  local copies, waits for them, and re-layouts  1.94 us (3%)
    pallas_call x1, Pallas kernels, exchange(): pl.pallas_call(exchange_kernel, out_shape=(jax.ShapeDtypeStruct((1, 512,...  61.8 us
    unnamed x2, local copies, waits for them, and re-layouts  1.94 us

profile of v2, /device:TPU:64, one launch (start us, length us, event | category | flops | bytes accessed | tf_op | source)
XLA Modules:
  0.0 64.4 jit_solution(11503342271416482390)
XLA Ops:
  0.6 61.8 %exchange.1 = (f32[1,512,512]{2,1,0:T(8,128)S(1)}, f32[1,512,512]{2,1,0:T(8,128)S(1)}) custom-call(f32[512,512]{1,0:T(8,128)} %x_hbm.1, f32[1824,256]{1,0:T(8,128)} %constant.2.clone.table_hbm), custom_call_target="tpu_custom_call" | custom-call | tf_op jit(solution)/shard_map/exchange/pallas_call | solution.py:245
  62.4 1.0 %copy.6 = f32[1,512,512]{2,1,0:T(8,128)} copy(f32[1,512,512]{2,1,0:T(8,128)S(1)} %get-tuple-element.4) | data formatting | bytes 2097152
  63.4 1.0 %copy.7 = f32[1,512,512]{2,1,0:T(8,128)} copy(f32[1,512,512]{2,1,0:T(8,128)S(1)} %get-tuple-element.5) | data formatting | bytes 2097152

commit v3 on v2

--- a/solution.py
+++ b/solution.py
@@ -10,11 +10,12 @@
 AXES = ("gx", "gy", "gz")
 STEPS = 131072
 F32, BF16 = jnp.float32, jnp.bfloat16
-Z_ORDER = [(d * s, c) for d in (1, 2, 3) for c in (0, 1) for s in (1, -1)] + [(4, 0), (4, 1), (0, 1)]
+Z_ORDER = [(0, 1), (4, 1), (4, 0), (-3, 1), (3, 1), (-3, 0), (3, 0), (-2, 1), (2, 1), (-2, 0), (2, 0), (-1, 1), (1, 1), (-1, 0), (1, 0)]
 XY_ORDER = [
     (1, 0), (-1, 0), (0, 1), (0, -1), (1, 1), (-1, -1), (1, -1), (-1, 1),
     (2, 1), (1, 2), (2, -1), (-1, 2), (2, 0), (0, 2), (2, 2),
 ]
+XY_ORDER = XY_ORDER[::-1]
 
 
 def tables():

time: 65.6 us -> 61.5 us (0.938)
  the two profiles are of different devices: /device:TPU:64 before, /device:TPU:1 now
where the time goes in v3:
time: 61.5 us; the launch traced here: 61.4 us
  Pallas kernels  58.8 us (96%)
  local copies, waits for them, and re-layouts  1.94 us (3%)
  between operations  0.64 us (1%)
    pallas_call x1, Pallas kernels, exchange(): pl.pallas_call(exchange_kernel, out_shape=(jax.ShapeDtypeStruct((1, 512,...  58.8 us
    unnamed x2, local copies, waits for them, and re-layouts  1.94 us

profile of v3, /device:TPU:1, one launch (start us, length us, event | category | flops | bytes accessed | tf_op | source)
XLA Modules:
  0.0 61.4 jit_solution(14599458871482542251)
XLA Ops:
  0.6 58.8 %exchange.1 = (f32[1,512,512]{2,1,0:T(8,128)S(1)}, f32[1,512,512]{2,1,0:T(8,128)S(1)}) custom-call(f32[512,512]{1,0:T(8,128)} %x_hbm.1, f32[1824,256]{1,0:T(8,128)} %constant.2.clone.table_hbm), custom_call_target="tpu_custom_call" | custom-call | tf_op jit(solution)/shard_map/exchange/pallas_call | solution.py:246
  59.5 1.0 %copy.6 = f32[1,512,512]{2,1,0:T(8,128)} copy(f32[1,512,512]{2,1,0:T(8,128)S(1)} %get-tuple-element.4) | data formatting | bytes 2097152
  60.4 1.0 %copy.7 = f32[1,512,512]{2,1,0:T(8,128)} copy(f32[1,512,512]{2,1,0:T(8,128)S(1)} %get-tuple-element.5) | data formatting | bytes 2097152

commit v4 on v3

--- a/solution.py
+++ b/solution.py
@@ -1,3 +1,5 @@
+import functools
+
 import jax
 import jax.numpy as jnp
 import numpy as np
@@ -58,11 +60,36 @@
     return one(a[0], b[0]) + (one(a[0], b[1]) + one(a[1], b[0]))
 
 
+SCALING = 1.0 / (float(STEPS) * 256.0)
+NT = ((1,), (1,))
+BOTH, RE, IM = pl.ds(0, 512), pl.ds(0, 256), pl.ds(256, 256)
+
+
+def modes_of(plain, block, lanes):
+    rows = pl.ds(256 * block, 256)
+    return plain[0, rows, lanes], plain[1, rows, lanes]
+
+
+def power_block(plain, i, j):
+    return product(modes_of(plain, i, BOTH), modes_of(plain, j, BOTH), NT) * SCALING
+
+
+def cross_block(plain, i, j):
+    cross = product(modes_of(plain, i, IM), modes_of(plain, j, RE), NT)
+    other = cross.T if i == j else product(modes_of(plain, i, RE), modes_of(plain, j, IM), NT)
+    return (cross - other) * SCALING
+
+
 def exchange_kernel(
-    x_hbm, table_hbm, power, cross,
-    x_in, table, high, low, send1, mid1, recv1, send2, mid2, out, plain, turned_w,
+    x_hbm, table_hbm, power, cross, plain,
+    x_in, table, high, low, send1, mid1, recv1, send2, mid2, out,
     load_sem, z_send, z_recv, xy_send, xy_recv, own_sem,
 ):
+    load_x = []
+    for h in range(2):
+        columns = pl.ds(256 * h, 256)
+        load_x.append(pltpu.make_async_copy(x_hbm.at[:, columns], x_in.at[:, columns], load_sem.at[h]))
+        load_x[h].start()
     y = lax.axis_index("gx")
     gy, gz = lax.axis_index("gy"), lax.axis_index("gz")
     z_hi, core = gy // 2, gy % 2
@@ -79,23 +106,30 @@
         px, py = (x + dx + 4) % 4, (y + dy + 4) % 4
         xy_peers.append((px % 2 * 8 + px // 2 * 4 + py, (py, gy, z_lo * 4 + px)))
 
-    load_x = pltpu.make_async_copy(x_hbm, x_in, load_sem.at[0])
-    load_x.start()
     barrier = pltpu.get_barrier_semaphore()
     for _, peer in z_peers + xy_peers:
         pl.semaphore_signal(barrier, inc=1, device_id=peer, device_id_type=MESH)
-    load_table = pltpu.make_async_copy(table_hbm, table, load_sem.at[1])
+    load_table = pltpu.make_async_copy(table_hbm, table, load_sem.at[2])
     load_table.start()
 
     def over_z(source, target, stage, h, target_outer):
         k = stage * 2 + h
         def place(ref):
             return ref.at[h, my_zc] if target_outer else ref.at[h, :, my_zc]
-        for zc, peer in z_peers:
+        def send(zc, peer):
             pltpu.make_async_remote_copy(
                 src_ref=source.at[h, :, zc], dst_ref=place(target), send_sem=z_send.at[k], recv_sem=z_recv.at[k],
                 device_id=peer, device_id_type=MESH,
             ).start()
+
+        if k == 3:
+            for pz in (0, 1, 2, 3, 7, 6, 4, 5):
+                for pc in (1 - core, core):
+                    zc = pz * 2 + pc
+                    pl.when(zc != my_zc)(functools.partial(send, zc, (y, pz // 4 * 2 + pc, pz % 4 * 4 + x)))
+        else:
+            for zc, peer in z_peers:
+                send(zc, peer)
         pltpu.make_async_copy(source.at[h, :, my_zc], place(target), own_sem.at[k]).start()
 
     def over_xy(source, target, stage, h, source_outer):
@@ -119,15 +153,17 @@
         pltpu.make_async_copy(one, one, own_sem.at[k if is_z else 4 + k]).wait()
 
     flat1 = send1.reshape(2048, 128)
-    load_x.wait()
-    for h in range(2):
+    def turn(h):
+        load_x[h].wait()
         for k in (2 * h, 2 * h + 1):
             for q in range(4):
                 turned = x_in[pl.ds(128 * q, 128), pl.ds(128 * k, 128)].T
                 flat1[pl.ds(512 * k + q, 128, stride=4), :] = turned
+
+    turn(0)
     pl.semaphore_wait(barrier, 30)
-
     over_z(send1, mid1, 0, 0, True)
+    turn(1)
     over_xy(send1, mid1, 0, 1, True)
     load_table.wait()
     for i in range(5):
@@ -211,31 +247,13 @@
             place = pl.ds(128 * q, 128)
             plain[0, here, place] = high
             plain[1, here, place] = low
-            place = pl.ds(128 * ((q + 2) % 4), 128)
-            turned_w[0, here, place] = high if q >= 2 else -high
-            turned_w[1, here, place] = low if q >= 2 else -low
-
-    nt = ((1,), (1,))
-    scaling = 1.0 / (float(STEPS) * 256.0)
-
-    def block(i, j):
-        a, b = pl.ds(256 * i, 256), pl.ds(256 * j, 256)
-        right = (plain[0, b, :], plain[1, b, :])
-        p = product((plain[0, a, :], plain[1, a, :]), right, nt) * scaling
-        c = product((turned_w[0, a, :], turned_w[1, a, :]), right, nt) * scaling
-        power[0, a, b] = p
-        cross[0, a, b] = c
-        if i != j:
-            power[0, b, a] = p.T
-            cross[0, b, a] = -c.T
 
     wait(out, 1, 0, False)
     spread(0)
-    block(0, 0)
+    power[...] = power_block(plain, 0, 0)
+    cross[...] = cross_block(plain, 0, 0)
     wait(out, 1, 1, True)
     spread(1)
-    block(0, 1)
-    block(1, 1)
 
 
 def exchange(currents):
@@ -245,25 +263,60 @@
     dma = pltpu.SemaphoreType.DMA
     return pl.pallas_call(
         exchange_kernel,
-        out_shape=(jax.ShapeDtypeStruct((1, 512, 512), F32),) * 2,
+        out_shape=(jax.ShapeDtypeStruct((256, 256), F32),) * 2 + (jax.ShapeDtypeStruct((2, 512, 512), BF16),),
         in_specs=[anywhere] * 2,
-        out_specs=(pl.BlockSpec(memory_space=pltpu.VMEM),) * 2,
+        out_specs=(pl.BlockSpec(memory_space=pltpu.VMEM),) * 3,
         scratch_shapes=[
             pltpu.VMEM((512, 512), F32),
             pltpu.VMEM(table.shape, F32),
             pltpu.VMEM((1280, 256), BF16),
             pltpu.VMEM((1280, 256), BF16),
             buffer, buffer, buffer, buffer, buffer, buffer,
-            pltpu.VMEM((2, 512, 512), BF16), pltpu.VMEM((2, 512, 512), BF16),
-            dma((2,)), dma((4,)), dma((4,)), dma((4,)), dma((4,)), dma((8,)),
+            dma((3,)), dma((4,)), dma((4,)), dma((4,)), dma((4,)), dma((8,)),
         ],
-        compiler_params=pltpu.CompilerParams(collective_id=0, has_side_effects=True, vmem_limit_bytes=51 * 1024 * 1024),
+        compiler_params=pltpu.CompilerParams(collective_id=0, has_side_effects=True, vmem_limit_bytes=54001664),
         name="exchange",
     )(currents, table)
 
 
+def finish_kernel(power00, cross00, plain, power, cross, blocks, sem):
+    copies = []
+
+    def put(source, target, i, j):
+        place = target.at[0, pl.ds(256 * i, 256), pl.ds(256 * j, 256)]
+        copies.append(pltpu.make_async_copy(source, place, sem.at[len(copies)]))
+        copies[-1].start()
+
+    put(power00, power, 0, 0)
+    put(cross00, cross, 0, 0)
+    blocks[0] = power_block(plain, 0, 1)
+    put(blocks.at[0], power, 0, 1)
+    blocks[1] = blocks[0].T
+    put(blocks.at[1], power, 1, 0)
+    blocks[2] = cross_block(plain, 0, 1)
+    put(blocks.at[2], cross, 0, 1)
+    blocks[3] = -blocks[2].T
+    put(blocks.at[3], cross, 1, 0)
+    blocks[4] = power_block(plain, 1, 1)
+    put(blocks.at[4], power, 1, 1)
+    blocks[5] = cross_block(plain, 1, 1)
+    put(blocks.at[5], cross, 1, 1)
+    for copy in copies:
+        copy.wait()
+
+
 def on_device(currents):
-    return exchange(currents)
+    here = pl.BlockSpec(memory_space=pltpu.VMEM)
+    shape = jax.ShapeDtypeStruct((1, 512, 512), F32)
+    return pl.pallas_call(
+        finish_kernel,
+        out_shape=(shape, shape),
+        in_specs=[here] * 3,
+        out_specs=(pl.BlockSpec(memory_space=pltpu.HBM),) * 2,
+        scratch_shapes=[pltpu.VMEM((6, 256, 256), F32), pltpu.SemaphoreType.DMA((8,))],
+        compiler_params=pltpu.CompilerParams(vmem_limit_bytes=8 * 1024 * 1024),
+        name="finish",
+    )(*exchange(currents))
 
 
 def solution(mesh):

time: 61.5 us -> 59.3 us (0.964)
  the two profiles are of different devices: /device:TPU:1 before, /device:TPU:64 now
where the time goes in v4:
time: 59.3 us; the launch traced here: 59.2 us
  Pallas kernels  58.6 us (99%)
  between operations  0.64 us (1%)
    pallas_call x1, Pallas kernels, exchange(): pl.pallas_call(exchange_kernel, out_shape=(jax.ShapeDtypeStruct((256, 256...  56.8 us
    pallas_call x1, Pallas kernels, on_device(): pl.pallas_call(finish_kernel, out_shape=(shape, shape), in_specs=[here] *...  1.81 us

profile of v4, /device:TPU:64, one launch (start us, length us, event | category | flops | bytes accessed | tf_op | source)
XLA Modules:
  0.0 59.2 jit_solution(16701288182117884791)
XLA Ops:
  0.6 56.8 %exchange.1 = (f32[256,256]{1,0:T(8,128)S(1)}, f32[256,256]{1,0:T(8,128)S(1)}, bf16[2,512,512]{2,1,0:T(8,128)(2,1)S(1)}) custom-call(f32[512,512]{1,0:T(8,128)} %x_hbm.1, f32[1824,256]{1,0:T(8,128)} %constant.2.clone.table_hbm), custom_call_target="tpu_custom_call" | custom-call | tf_op jit(solution)/shard_map/exchange/pallas_call | solution.py:264
  57.4 1.8 %finish.1 = (f32[1,512,512]{2,1,0:T(8,128)}, f32[1,512,512]{2,1,0:T(8,128)}) custom-call(f32[256,256]{1,0:T(8,128)S(1)} %get-tuple-element.5.power00, f32[256,256]{1,0:T(8,128)S(1)} %get-tuple-element.6.cross00, bf16[2,512,512]{2,1,0:T(8,128)(2,1)S(1)} %get-tuple-element.7.plain), custom_call_target="tpu_custom_call" | custom-call | tf_op jit(solution)/shard_map/finish/pallas_call | solution.py:311

commit v5 on v4

--- a/solution.py
+++ b/solution.py
@@ -98,12 +98,13 @@
     my_zc = z * 2 + core
     my_xy = x % 2 * 8 + x // 2 * 4 + y
     z_peers, xy_peers = [], []
+    way = 1 - 2 * core
     for dz, dc in Z_ORDER:
-        pz = (z + dz + 8) % 8
+        pz = (z + dz * way + 8) % 8
         pc = 1 - core if dc else core
         z_peers.append((pz * 2 + pc, (y, pz // 4 * 2 + pc, pz % 4 * 4 + x)))
     for dx, dy in XY_ORDER:
-        px, py = (x + dx + 4) % 4, (y + dy + 4) % 4
+        px, py = (x + dx * way + 4) % 4, (y + dy * way + 4) % 4
         xy_peers.append((px % 2 * 8 + px // 2 * 4 + py, (py, gy, z_lo * 4 + px)))
 
     barrier = pltpu.get_barrier_semaphore()
@@ -122,8 +123,8 @@
                 device_id=peer, device_id_type=MESH,
             ).start()
 
-        if k == 3:
-            for pz in (0, 1, 2, 3, 7, 6, 4, 5):
+        if k >= 2:
+            for pz in ((0, 1, 2, 7, 3, 6, 4, 5) if h else (0, 1, 2, 3, 7, 6, 4, 5)):
                 for pc in (1 - core, core):
                     zc = pz * 2 + pc
                     pl.when(zc != my_zc)(functools.partial(send, zc, (y, pz // 4 * 2 + pc, pz % 4 * 4 + x)))
@@ -145,12 +146,16 @@
 
     def wait(target, stage, h, is_z):
         k = stage * 2 + h
-        send, recv = (z_send, z_recv) if is_z else (xy_send, xy_recv)
         some = target.at[h, pl.ds(0, 15)]
-        pltpu.make_async_copy(some, some, recv.at[k]).wait()
-        pltpu.make_async_copy(some, some, send.at[k]).wait()
+        pltpu.make_async_copy(some, some, (z_recv if is_z else xy_recv).at[k]).wait()
         one = target.at[h, 0]
         pltpu.make_async_copy(one, one, own_sem.at[k if is_z else 4 + k]).wait()
+
+    def drain():
+        for k in range(4):
+            for sem in (z_send, xy_send):
+                some = mid1.at[0, pl.ds(0, 15)]
+                pltpu.make_async_copy(some, some, sem.at[k]).wait()
 
     flat1 = send1.reshape(2048, 128)
     def turn(h):
@@ -254,6 +259,7 @@
     cross[...] = cross_block(plain, 0, 0)
     wait(out, 1, 1, True)
     spread(1)
+    drain()
 
 
 def exchange(currents):

time: 59.3 us -> 59.3 us (level)
  no operation moved by 1% of the time
where the time goes in v5:
time: 59.3 us; the launch traced here: 59.2 us
  Pallas kernels  58.6 us (99%)
  between operations  0.64 us (1%)
    pallas_call x1, Pallas kernels, exchange(): pl.pallas_call(exchange_kernel, out_shape=(jax.ShapeDtypeStruct((256, 256...  56.8 us
    pallas_call x1, Pallas kernels, on_device(): pl.pallas_call(finish_kernel, out_shape=(shape, shape), in_specs=[here] *...  1.81 us

profile of v5, /device:TPU:64, one launch (start us, length us, event | category | flops | bytes accessed | tf_op | source)
XLA Modules:
  0.0 59.2 jit_solution(5084403088980195888)
XLA Ops:
  0.6 56.8 %exchange.1 = (f32[256,256]{1,0:T(8,128)S(1)}, f32[256,256]{1,0:T(8,128)S(1)}, bf16[2,512,512]{2,1,0:T(8,128)(2,1)S(1)}) custom-call(f32[512,512]{1,0:T(8,128)} %x_hbm.1, f32[1824,256]{1,0:T(8,128)} %constant.2.clone.table_hbm), custom_call_target="tpu_custom_call" | custom-call | tf_op jit(solution)/shard_map/exchange/pallas_call | solution.py:270
  57.4 1.8 %finish.1 = (f32[1,512,512]{2,1,0:T(8,128)}, f32[1,512,512]{2,1,0:T(8,128)}) custom-call(f32[256,256]{1,0:T(8,128)S(1)} %get-tuple-element.5.power00, f32[256,256]{1,0:T(8,128)S(1)} %get-tuple-element.6.cross00, bf16[2,512,512]{2,1,0:T(8,128)(2,1)S(1)} %get-tuple-element.7.plain), custom_call_target="tpu_custom_call" | custom-call | tf_op jit(solution)/shard_map/finish/pallas_call | solution.py:317

commit v6 on v4

--- a/solution.py
+++ b/solution.py
@@ -136,11 +136,19 @@
         k = stage * 2 + h
         def piece(xy):
             return source.at[h, xy] if source_outer else source.at[h, :, xy]
-        for xy, peer in xy_peers:
+        def send(xy, peer):
             pltpu.make_async_remote_copy(
                 src_ref=piece(xy), dst_ref=target.at[h, my_xy], send_sem=xy_send.at[k], recv_sem=xy_recv.at[k],
                 device_id=peer, device_id_type=MESH,
             ).start()
+
+        if k == 2:
+            for px, py in sorted(((i, j) for i in range(4) for j in range(4)), key=sum):
+                xy = px % 2 * 8 + px // 2 * 4 + py
+                pl.when(xy != my_xy)(functools.partial(send, xy, (py, gy, z_lo * 4 + px)))
+        else:
+            for xy, peer in xy_peers:
+                send(xy, peer)
         pltpu.make_async_copy(piece(my_xy), target.at[h, my_xy], own_sem.at[4 + k]).start()
 
     def wait(target, stage, h, is_z):

time: 59.3 us -> 59.3 us (level)
  no operation moved by 1% of the time
where the time goes in v6:
time: 59.3 us; the launch traced here: 59.2 us
  Pallas kernels  58.6 us (99%)
  between operations  0.64 us (1%)
    pallas_call x1, Pallas kernels, exchange(): pl.pallas_call(exchange_kernel, out_shape=(jax.ShapeDtypeStruct((256, 256...  56.8 us
    pallas_call x1, Pallas kernels, on_device(): pl.pallas_call(finish_kernel, out_shape=(shape, shape), in_specs=[here] *...  1.81 us

profile of v6, /device:TPU:64, one launch (start us, length us, event | category | flops | bytes accessed | tf_op | source)
XLA Modules:
  0.0 59.2 jit_solution(234806599147926177)
XLA Ops:
  0.6 56.8 %exchange.1 = (f32[256,256]{1,0:T(8,128)S(1)}, f32[256,256]{1,0:T(8,128)S(1)}, bf16[2,512,512]{2,1,0:T(8,128)(2,1)S(1)}) custom-call(f32[512,512]{1,0:T(8,128)} %x_hbm.1, f32[1824,256]{1,0:T(8,128)} %constant.2.clone.table_hbm), custom_call_target="tpu_custom_call" | custom-call | tf_op jit(solution)/shard_map/exchange/pallas_call | solution.py:272
  57.4 1.8 %finish.1 = (f32[1,512,512]{2,1,0:T(8,128)}, f32[1,512,512]{2,1,0:T(8,128)}) custom-call(f32[256,256]{1,0:T(8,128)S(1)} %get-tuple-element.5.power00, f32[256,256]{1,0:T(8,128)S(1)} %get-tuple-element.6.cross00, bf16[2,512,512]{2,1,0:T(8,128)(2,1)S(1)} %get-tuple-element.7.plain), custom_call_target="tpu_custom_call" | custom-call | tf_op jit(solution)/shard_map/finish/pallas_call | solution.py:319
